TPU v7x, 128 devices: a whole 4x4x4 slice. The times are simulated.
128 devices in a mesh: row: 8 (over y_lo, z), col: 16 (over x, y_hi, core).
Axes of the slice: x: 4, y: 4 (y_hi: 2, y_lo: 2; y = y_hi * 2 + y_lo), z: 4, core: 2. Of those that a mesh axis runs over, the one named last changes fastest.
Arguments:
- inverse: float32 [16384, 16384], P('row', 'col'), may hold values from -0.0625 to 0.0625
- pattern: int32 [128, 128], P('row', 'col'), may hold values 0 or 1
- factor_first: float32 [16384, 256], P('col'), may hold values from -1.5 to 1.5
- factor_second: float32 [16384, 256], P('col'), may hold values from -1.5 to 1.5
- rows_first: int32 [64], replicated, may hold values from 0 to 127, as said below
- rows_second: int32 [64], replicated, may hold values from 0 to 127, as said below
- coupling: float32 [256, 256], replicated, may hold values from -0.375 to 0.375
- diag_first: float32 [256, 256], replicated, may hold values from -6 to 6
- diag_second: float32 [256, 256], replicated, may hold values from -6 to 6
Outputs:
- panel_one: float32 [16384, 256], P(('row', 'col'))
- panel_two: float32 [16384, 256], P(('row', 'col'))
- block_one: float32 [256, 256], replicated
- block_cross: float32 [256, 256], replicated
- block_two: float32 [256, 256], replicated
Inputs may be any that keep to these rules, and one draw needn't show every extreme that they name: `rows_first`: 64 distinct block indices in increasing order; the first block, the block 64 and the last block are always among them. `rows_second`: 64 distinct block indices in increasing order; the first block, the block 64 and the last block are always among them.
All inputs are finite; a program needn't handle non-finite values. No bound on the sum of `pattern` on one device may be relied on, other than what follows from the above.
Results may differ from a plain program's by a relative error of at most 0.000071.
Values sent between devices are 32-bit elements; how exact they have to be, the bound alone decides.
A program may use at most 128 MiB of HBM per device.

v0:
```python
import jax
import jax.numpy as jnp
from jax import lax
from jax.sharding import PartitionSpec as P

BLK = 128


def member(block_ids, rows_list):
    hits = (block_ids[:, None] == rows_list[None, :]).astype(jnp.float32)
    return jnp.sum(hits, axis=1)


def per_device(
    inverse,
    pattern,
    factor_first,
    factor_second,
    rows_first,
    rows_second,
    coupling,
    diag_first,
    diag_second,
):
    high = lax.Precision.HIGHEST
    col_count = lax.axis_size("col")
    row_index = lax.axis_index("row")
    col_index = lax.axis_index("col")
    share_rows = factor_first.shape[0]
    local_rows, local_cols = inverse.shape
    quota_rows = local_rows // col_count
    masked = (
        inverse.reshape(local_rows // BLK, BLK, local_cols // BLK, BLK)
        * pattern.astype(jnp.float32)[:, None, :, None]
    ).reshape(local_rows, local_cols)
    share_ids = (col_index * share_rows + jnp.arange(share_rows, dtype=jnp.int32)) // BLK
    own_start = (row_index * col_count + col_index) * quota_rows
    own_ids = (own_start + jnp.arange(quota_rows, dtype=jnp.int32)) // BLK

    def fetch_rows(factor):
        gathered = lax.all_gather(factor, "col", axis=0, tiled=True)
        return lax.dynamic_slice_in_dim(gathered, own_start, quota_rows, 0)

    def panel_product(factor_kept):
        return lax.psum_scatter(
            jnp.dot(masked, factor_kept, precision=high), "col", scatter_dimension=0, tiled=True
        )

    x_one = factor_first * member(share_ids, rows_first)[:, None]
    x_two = factor_second * member(share_ids, rows_second)[:, None]
    panel_one = -panel_product(x_one)
    near_one = fetch_rows(factor_first)
    near_one = near_one * member(own_ids, rows_first)[:, None]
    first_total = lax.psum(jnp.dot(near_one.T, panel_one, precision=high), ("row", "col"))
    block_one = diag_first - first_total
    near_two = fetch_rows(factor_second)
    near_two = near_two * member(own_ids, rows_second)[:, None]
    panel_two = -(panel_product(x_two) + jnp.dot(panel_one, coupling, precision=high))
    cross_sum, quad_sum = lax.psum(
        (
            jnp.dot(panel_one.T, near_two, precision=high),
            jnp.dot(near_two.T, panel_two, precision=high),
        ),
        ("row", "col"),
    )
    block_cross = -(cross_sum + jnp.dot(block_one, coupling, precision=high))
    block_two = diag_second - quad_sum - jnp.dot(coupling.T, block_cross, precision=high)
    return (panel_one, panel_two, block_one, block_cross, block_two)


def solution(mesh):
    return jax.shard_map(
        per_device,
        mesh=mesh,
        in_specs=(
            P("row", "col"),
            P("row", "col"),
            P("col", None),
            P("col", None),
            P(),
            P(),
            P(),
            P(),
            P(),
        ),
        out_specs=(P(("row", "col"), None), P(("row", "col"), None), P(), P(), P()),
        check_vma=False,
    )
```

profile of v0, /device:TPU:1, one launch (start us, length us, event | category | flops | bytes accessed | tf_op | source)
XLA Modules:
  0.0 555.6 jit_solution(4285565588301605714)
XLA Ops:
  7.2 0.0 copy-start
  7.2 0.0 reduce-scatter.3.cloned.1.call-start
  7.2 0.7 convert_element_type.15
  7.9 0.1 copy.16
  8.0 1.0 convert_reduce_fusion
  9.0 0.6 mul.52
  9.6 0.0 copy-start.1
  9.6 3.8 copy-done.1
  13.4 0.1 copy-done.2
  13.5 10.3 %fusion.1 = f32[2048,256]{1,0:T(8,128)} fusion(f32[2048,1024]{1,0:T(8,128)S(1)} %copy-done.2, f32[256,8,8,128]{3,2,1,0:T(8,128)S(1)} %bitcast.19, f32[1024,256]{1,0:T(8,128)} %param.11, f32[1024]{0:T(1024)S(1)} %get-tuple-element.6), kind=kOutput, calls=%fused_computation.2 | convolution fusion | flops 6444810240 | bytes 19927040 | tf_op jit(solution)/shard_map/dot_general | solution.py:46
  23.8 0.0 reduce-scatter.3.cloned.1.call-update
  23.8 0.2 reduce-scatter.5.cloned.1.call-start
  24.0 0.0 copy-done.3
  24.0 0.0 copy-start.10
  24.0 0.0 copy-start.11
  24.1 0.0 copy-start.8
  24.1 12.9 %fusion = f32[2048,256]{1,0:T(8,128)} fusion(f32[2048,1024]{1,0:T(8,128)} %param.9, f32[256,8,8,128]{3,2,1,0:T(8,128)} %bitcast.20, f32[1024,256]{1,0:T(8,128)S(1)} %copy-done.3, f32[1024]{0:T(1024)S(1)} %get-tuple-element.5), kind=kOutput, calls=%fused_computation.1 | convolution fusion | flops 6444810240 | bytes 19927040 | tf_op jit(solution)/shard_map/dot_general | solution.py:46
  36.9 0.0 reduce-scatter.5.cloned.1.call-update
  37.0 0.0 all-gather.5.cloned.1.call-start
  37.0 0.7 all-gather.5.cloned.1.call-update
  37.7 0.0 all-gather.3.cloned.1.call-start
  37.8 0.5 all-gather.3.cloned.1.call-update
  38.3 0.0 all-reduce.3.cloned.1.call-start
  38.4 0.0 copy-done.10
  38.4 0.0 copy-done.11
  38.4 0.1 convert_reduce_fusion.2
  38.5 57.6 %reduce-scatter.3.cloned.1.call-done = f32[128,256]{1,0:T(8,128)} async-done(((f32[2048,256]{1,0:T(8,128)}), f32[128,256]{1,0:T(8,128)}) %reduce-scatter.3.cloned.1.call-update) | async-done | bytes 131088 | tf_op jit(solution)/shard_map/reduce_scatter | solution.py:45
  96.1 0.9 neg.9
  97.0 0.0 copy-start.4
  97.0 73.0 %reduce-scatter.5.cloned.1.call-done = f32[128,256]{1,0:T(8,128)} async-done(((f32[2048,256]{1,0:T(8,128)}), f32[128,256]{1,0:T(8,128)}) %reduce-scatter.5.cloned.1.call-update) | async-done | bytes 131088 | tf_op jit(solution)/shard_map/reduce_scatter | solution.py:45
  170.0 0.0 copy-done
  170.0 1.2 fusion.4
  171.2 0.0 copy-start.7
  171.2 112.4 %all-gather.5.cloned.1.call-done = f32[16384,256]{1,0:T(8,128)} async-done(((f32[1024,256]{1,0:T(8,128)}), f32[16384,256]{1,0:T(8,128)}) %all-gather.5.cloned.1.call-update) | async-done | bytes 16777232 | tf_op jit(solution)/shard_map/all_gather | solution.py:41
  283.5 2.1 fusion.13
  285.6 2.1 fusion.12
  287.7 105.6 %all-gather.3.cloned.1.call-done = f32[16384,256]{1,0:T(8,128)} async-done(((f32[1024,256]{1,0:T(8,128)}), f32[16384,256]{1,0:T(8,128)}) %all-gather.3.cloned.1.call-update) | async-done | bytes 16777232 | tf_op jit(solution)/shard_map/all_gather | solution.py:41
  393.3 2.1 fusion.9
  395.3 0.0 all-reduce.3.cloned.1.call-update
  395.4 148.9 %all-reduce.3.cloned.1.call-done = (f32[256,256]{1,0:T(8,128)}, f32[256,256]{1,0:T(8,128)}, f32[256,256]{1,0:T(8,128)}) async-done(((f32[256,256]{1,0:T(8,128)}, f32[256,256]{1,0:T(8,128)}, f32[256,256]{1,0:T(8,128)}), (f32[256,256]{1,0:T(8,128)}, f32[256,256]{1,0:T(8,128)}, f32[256,256]{1,0:T(8,128)})) %all-reduce.3.cloned.1.call-update) | async-done | bytes 786448 | tf_op jit(solution)/shard_map/psum | solution.py:54
  544.3 0.0 copy-done.8
  544.3 1.0 sub.23
  545.2 0.0 copy-start.5
  545.3 1.4 fusion.3
  546.7 0.0 copy-start.6
  546.7 0.0 copy-done.9
  546.7 2.3 fusion.2
  549.1 0.0 copy-done.6
  (8 shorter events, 0.0 us)
Async XLA Ops:
  7.2 162.8 %copy-start = (f32[256,256]{1,0:T(8,128)S(1)}, f32[256,256]{1,0:T(8,128)}, u32[]{:S(2)}) copy-start(f32[256,256]{1,0:T(8,128)} %param.15) | copy-start | bytes 786436
  7.2 88.9 %reduce-scatter.3.cloned.1.call-start = ((), (), s32[]{:S(2)}) async-start(), calls=%async_computation.2 | async-start | bytes 2228224 | tf_op jit(solution)/shard_map/reduce_scatter | solution.py:45
  8.0 5.5 copy-start.2
  9.6 3.8 copy-start.1
  13.5 10.5 %copy-start.3 = (f32[1024,256]{1,0:T(8,128)S(1)}, f32[1024,256]{1,0:T(8,128)}, u32[]{:S(2)}) copy-start(f32[1024,256]{1,0:T(8,128)} %param.12) | copy-start | bytes 3145732
  23.8 146.2 %reduce-scatter.5.cloned.1.call-start = ((), (), s32[]{:S(2)}) async-start(), calls=%async_computation.3 | async-start | bytes 2228224 | tf_op jit(solution)/shard_map/reduce_scatter | solution.py:45
  24.0 14.3 %copy-start.10 = (s32[64]{0:T(128)S(1)}, s32[64]{0:T(128)}, u32[]{:S(2)}) copy-start(s32[64]{0:T(128)} %param.14) | copy-start | bytes 772
  24.0 14.3 %copy-start.11 = (s32[64]{0:T(128)S(1)}, s32[64]{0:T(128)}, u32[]{:S(2)}) copy-start(s32[64]{0:T(128)} %param.13) | copy-start | bytes 772
  24.1 520.2 %copy-start.8 = (f32[256,256]{1,0:T(8,128)S(1)}, f32[256,256]{1,0:T(8,128)}, u32[]{:S(2)}) copy-start(f32[256,256]{1,0:T(8,128)} %param.16) | copy-start | bytes 786436
  36.9 509.8 %copy-start.9 = (f32[256,256]{1,0:T(8,128)S(1)}, f32[256,256]{1,0:T(8,128)}, u32[]{:S(2)}) copy-start(f32[256,256]{1,0:T(8,128)} %param.17) | copy-start | bytes 786436
  37.0 246.6 %all-gather.5.cloned.1.call-start = ((), (), s32[]{:S(2)}) async-start(), calls=%async_computation.5 | async-start | bytes 17825792 | tf_op jit(solution)/shard_map/all_gather | solution.py:41
  37.7 355.5 %all-gather.3.cloned.1.call-start = ((), (), s32[]{:S(2)}) async-start(), calls=%async_computation.4 | async-start | bytes 17825792 | tf_op jit(solution)/shard_map/all_gather | solution.py:41
  38.3 506.0 %all-reduce.3.cloned.1.call-start = ((), (), s32[]{:S(2)}) async-start(), calls=%async_computation.6 | async-start | bytes 1572864 | tf_op jit(solution)/shard_map/psum | solution.py:54
  97.0 452.1 %copy-start.4 = (f32[128,256]{1,0:T(8,128)}, f32[128,256]{1,0:T(8,128)S(1)}, u32[]{:S(2)}) copy-start(f32[128,256]{1,0:T(8,128)S(1)} %neg.9) | copy-start | bytes 393220
  171.2 377.9 %copy-start.7 = (f32[128,256]{1,0:T(8,128)}, f32[128,256]{1,0:T(8,128)S(1)}, u32[]{:S(2)}) copy-start(f32[128,256]{1,0:T(8,128)S(1)} %fusion.4) | copy-start | bytes 393220
  545.2 3.8 copy-start.5
  546.7 2.4 copy-start.6
Sparse Core Ops, SparseCore 0:
  23.9 72.0 reduce-scatter.2
  100.0 69.9 reduce-scatter.4
  172.4 111.1 all-gather.4
  285.8 107.4 all-gather.2
  398.7 145.5 all-reduce.2
where the time goes:
time: 556 us
  waiting for transfers between devices  499 us (90%)
  matrix products  34.3 us (6%)
  between operations  14 us (3%)
    all_gather x2, waiting for transfers between devices, fetch_rows(): gathered = lax.all_gather(factor, 'col', axis=0, tiled=True)  218 us
    psum x1, waiting for transfers between devices, per_device(): lax.psum(jnp.dot(near_one.T, panel_one, precision=high), ('row', 'col'))  149 us
    reduce_scatter x2, waiting for transfers between devices, panel_product(): lax.psum_scatter(jnp.dot(masked, factor_kept, precision=high), 'col', sca...  131 us
    dot_general x2, matrix products, panel_product(): jnp.dot(masked, factor_kept, precision=high)  23.1 us
  transfers between devices with their start and end apart: 5, of which 5 were waited for; matrix products, arithmetic and copies ran while one was open for 3% of the time, Pallas kernels for 0%

commit v1 on v0

--- a/solution.py
+++ b/solution.py
@@ -1,9 +1,20 @@
+import functools
 import jax
 import jax.numpy as jnp
 from jax import lax
 from jax.sharding import PartitionSpec as P
+from jax.lax import psum
 
 BLK = 128
+
+
+def switch_the_boxes(payload, link_axis, net_axis):
+    for u in (link_axis, net_axis):
+        payload = psum(payload, axis_name=u)
+    return payload
+
+
+assign_the_space = functools.partial(switch_the_boxes, link_axis="row", net_axis="col")
 
 
 def member(block_ids, rows_list):
@@ -51,7 +62,7 @@
     panel_one = -panel_product(x_one)
     near_one = fetch_rows(factor_first)
     near_one = near_one * member(own_ids, rows_first)[:, None]
-    first_total = lax.psum(jnp.dot(near_one.T, panel_one, precision=high), ("row", "col"))
+    first_total = assign_the_space(jnp.dot(near_one.T, panel_one, precision=high))
     block_one = diag_first - first_total
     near_two = fetch_rows(factor_second)
     near_two = near_two * member(own_ids, rows_second)[:, None]

time: 556 us -> 773 us (1.39)
  waiting for transfers between devices: 499 us -> 715 us
    psum x1 -> x3, waiting for transfers between devices: 149 us -> 359 us  [the longest x2 207 us: switch_the_boxes(): payload = psum(payload, axis_name=u)]
    all_gather x2, waiting for transfers between devices: 218 us -> 229 us  [fetch_rows(): gathered = lax.all_gather(factor, 'col', axis=0, tiled=True)]
  transfers between devices with their start and end apart: 5 -> 7, of which waited for: 5 -> 7; matrix products, arithmetic and copies ran while one was open for 3% -> 3% of each run, Pallas kernels for 0% -> 0%
where the time goes in v1:
time: 773 us
  waiting for transfers between devices  715 us (92%)
  matrix products  34.1 us (4%)
  between operations  14.3 us (2%)
    all_gather x2, waiting for transfers between devices, fetch_rows(): gathered = lax.all_gather(factor, 'col', axis=0, tiled=True)  229 us
    psum x2, waiting for transfers between devices, switch_the_boxes(): payload = psum(payload, axis_name=u)  207 us
    psum x1, waiting for transfers between devices, per_device(): lax.psum((jnp.dot(panel_one.T, near_two, precision=high), jnp.dot(near_tw...  152 us
    reduce_scatter x2, waiting for transfers between devices, panel_product(): lax.psum_scatter(jnp.dot(masked, factor_kept, precision=high), 'col', sca...  126 us
    dot_general x2, matrix products, panel_product(): jnp.dot(masked, factor_kept, precision=high)  23.1 us
  transfers between devices with their start and end apart: 7, of which 7 were waited for; matrix products, arithmetic and copies ran while one was open for 3% of the time, Pallas kernels for 0%

profile of v1, /device:TPU:1, one launch (start us, length us, event | category | flops | bytes accessed | tf_op | source)
XLA Modules:
  0.0 772.5 jit_solution(7169947626777198687)
XLA Ops:
  7.2 0.0 copy-start
  7.2 0.0 reduce-scatter.3.cloned.1.call-start
  7.2 0.7 convert_element_type.15
  8.0 0.1 copy.16
  8.0 1.0 convert_reduce_fusion
  9.0 0.6 mul.52
  9.6 0.0 copy-start.1
  9.6 3.8 copy-done.1
  13.4 0.1 copy-done.2
  13.5 10.3 %fusion.1 = f32[2048,256]{1,0:T(8,128)} fusion(f32[2048,1024]{1,0:T(8,128)S(1)} %copy-done.2, f32[256,8,8,128]{3,2,1,0:T(8,128)S(1)} %bitcast.19, f32[1024,256]{1,0:T(8,128)} %param.11, f32[1024]{0:T(1024)S(1)} %get-tuple-element.6), kind=kOutput, calls=%fused_computation.2 | convolution fusion | flops 6444810240 | bytes 19927040 | tf_op jit(solution)/shard_map/dot_general | solution.py:57
  23.8 0.0 reduce-scatter.3.cloned.1.call-update
  23.8 0.0 all-gather.3.cloned.1.call-start
  23.8 0.7 all-gather.3.cloned.1.call-update
  24.5 0.2 reduce-scatter.5.cloned.1.call-start
  24.8 0.0 copy-start.10
  24.8 0.0 copy-start.11
  24.8 0.0 copy-start.8
  24.8 12.8 %fusion = f32[2048,256]{1,0:T(8,128)} fusion(f32[2048,1024]{1,0:T(8,128)} %param.9, f32[256,8,8,128]{3,2,1,0:T(8,128)} %bitcast.20, f32[1024,256]{1,0:T(8,128)S(1)} %copy-done.3, f32[1024]{0:T(1024)S(1)} %get-tuple-element.5), kind=kOutput, calls=%fused_computation.1 | convolution fusion | flops 6444810240 | bytes 19927040 | tf_op jit(solution)/shard_map/dot_general | solution.py:57
  37.6 0.0 reduce-scatter.5.cloned.1.call-update
  37.6 0.0 all-reduce.5.cloned.1.call-start
  37.7 0.1 convert_reduce_fusion.2
  37.8 58.2 %reduce-scatter.3.cloned.1.call-done = f32[128,256]{1,0:T(8,128)} async-done(((f32[2048,256]{1,0:T(8,128)}), f32[128,256]{1,0:T(8,128)}) %reduce-scatter.3.cloned.1.call-update) | async-done | bytes 131088 | tf_op jit(solution)/shard_map/reduce_scatter | solution.py:56
  96.0 0.9 neg.9
  96.9 0.0 copy-start.4
  96.9 112.6 %all-gather.3.cloned.1.call-done = f32[16384,256]{1,0:T(8,128)} async-done(((f32[1024,256]{1,0:T(8,128)}), f32[16384,256]{1,0:T(8,128)}) %all-gather.3.cloned.1.call-update) | async-done | bytes 16777232 | tf_op jit(solution)/shard_map/all_gather | solution.py:52
  209.6 2.1 fusion.9
  211.7 0.0 all-reduce.5.cloned.1.call-update
  211.7 0.0 all-gather.5.cloned.1.call-start
  211.7 0.5 all-gather.5.cloned.1.call-update
  212.3 0.0 all-reduce.7.cloned.1.call-start
  212.3 67.4 %reduce-scatter.5.cloned.1.call-done = f32[128,256]{1,0:T(8,128)} async-done(((f32[2048,256]{1,0:T(8,128)}), f32[128,256]{1,0:T(8,128)}) %reduce-scatter.5.cloned.1.call-update) | async-done | bytes 131088 | tf_op jit(solution)/shard_map/reduce_scatter | solution.py:56
  279.8 1.2 fusion.4
  281.0 0.0 copy-start.7
  281.0 72.5 %all-reduce.5.cloned.1.call-done = f32[256,256]{1,0:T(8,128)} async-done(((f32[256,256]{1,0:T(8,128)}), f32[256,256]{1,0:T(8,128)}) %all-reduce.5.cloned.1.call-update) | async-done | bytes 262160 | tf_op jit(solution)/shard_map/psum | solution.py:13
  353.4 0.0 all-reduce.7.cloned.1.call-update
  353.4 0.0 all-reduce.9.cloned.1.call-start
  353.5 116.7 %all-gather.5.cloned.1.call-done = f32[16384,256]{1,0:T(8,128)} async-done(((f32[1024,256]{1,0:T(8,128)}), f32[16384,256]{1,0:T(8,128)}) %all-gather.5.cloned.1.call-update) | async-done | bytes 16777232 | tf_op jit(solution)/shard_map/all_gather | solution.py:52
  470.2 2.1 fusion.13
  472.2 2.1 fusion.12
  474.3 0.0 all-reduce.9.cloned.1.call-update
  474.3 134.2 %all-reduce.7.cloned.1.call-done = f32[256,256]{1,0:T(8,128)} async-done(((f32[256,256]{1,0:T(8,128)}), f32[256,256]{1,0:T(8,128)}) %all-reduce.7.cloned.1.call-update) | async-done | bytes 262160 | tf_op jit(solution)/shard_map/psum | solution.py:13
  608.5 1.0 sub.23
  609.5 0.0 copy-start.5
  609.5 152.4 %all-reduce.9.cloned.1.call-done = (f32[256,256]{1,0:T(8,128)}, f32[256,256]{1,0:T(8,128)}) async-done(((f32[256,256]{1,0:T(8,128)}, f32[256,256]{1,0:T(8,128)}), (f32[256,256]{1,0:T(8,128)}, f32[256,256]{1,0:T(8,128)})) %all-reduce.9.cloned.1.call-update) | async-done | bytes 524304 | tf_op jit(solution)/shard_map/psum | solution.py:70
  761.9 1.3 fusion.3
  763.3 0.0 copy-start.6
  763.3 2.3 fusion.2
  765.6 0.0 copy-done.4
  (14 shorter events, 0.0 us)
Async XLA Ops:
  7.2 272.6 %copy-start = (f32[256,256]{1,0:T(8,128)S(1)}, f32[256,256]{1,0:T(8,128)}, u32[]{:S(2)}) copy-start(f32[256,256]{1,0:T(8,128)} %param.15) | copy-start | bytes 786436
  7.2 88.8 %reduce-scatter.3.cloned.1.call-start = ((), (), s32[]{:S(2)}) async-start(), calls=%async_computation.2 | async-start | bytes 2228224 | tf_op jit(solution)/shard_map/reduce_scatter | solution.py:56
  8.0 5.5 copy-start.2
  9.6 3.8 copy-start.1
  13.5 11.3 %copy-start.3 = (f32[1024,256]{1,0:T(8,128)S(1)}, f32[1024,256]{1,0:T(8,128)}, u32[]{:S(2)}) copy-start(f32[1024,256]{1,0:T(8,128)} %param.12) | copy-start | bytes 3145732
  23.8 185.8 %all-gather.3.cloned.1.call-start = ((), (), s32[]{:S(2)}) async-start(), calls=%async_computation.4 | async-start | bytes 17825792 | tf_op jit(solution)/shard_map/all_gather | solution.py:52
  24.5 255.2 %reduce-scatter.5.cloned.1.call-start = ((), (), s32[]{:S(2)}) async-start(), calls=%async_computation.3 | async-start | bytes 2228224 | tf_op jit(solution)/shard_map/reduce_scatter | solution.py:56
  24.8 12.9 %copy-start.10 = (s32[64]{0:T(128)S(1)}, s32[64]{0:T(128)}, u32[]{:S(2)}) copy-start(s32[64]{0:T(128)} %param.14) | copy-start | bytes 772
  24.8 12.9 %copy-start.11 = (s32[64]{0:T(128)S(1)}, s32[64]{0:T(128)}, u32[]{:S(2)}) copy-start(s32[64]{0:T(128)} %param.13) | copy-start | bytes 772
  24.8 583.7 %copy-start.8 = (f32[256,256]{1,0:T(8,128)S(1)}, f32[256,256]{1,0:T(8,128)}, u32[]{:S(2)}) copy-start(f32[256,256]{1,0:T(8,128)} %param.16) | copy-start | bytes 786436
  37.6 725.7 %copy-start.9 = (f32[256,256]{1,0:T(8,128)S(1)}, f32[256,256]{1,0:T(8,128)}, u32[]{:S(2)}) copy-start(f32[256,256]{1,0:T(8,128)} %param.17) | copy-start | bytes 786436
  37.6 315.8 %all-reduce.5.cloned.1.call-start = ((), (), s32[]{:S(2)}) async-start(), calls=%async_computation.5 | async-start | bytes 524288 | tf_op jit(solution)/shard_map/psum | solution.py:13
  96.9 668.7 %copy-start.4 = (f32[128,256]{1,0:T(8,128)}, f32[128,256]{1,0:T(8,128)S(1)}, u32[]{:S(2)}) copy-start(f32[128,256]{1,0:T(8,128)S(1)} %neg.9) | copy-start | bytes 393220
  211.7 258.5 %all-gather.5.cloned.1.call-start = ((), (), s32[]{:S(2)}) async-start(), calls=%async_computation.7 | async-start | bytes 17825792 | tf_op jit(solution)/shard_map/all_gather | solution.py:52
  212.3 396.2 %all-reduce.7.cloned.1.call-start = ((), (), s32[]{:S(2)}) async-start(), calls=%async_computation.6 | async-start | bytes 524288 | tf_op jit(solution)/shard_map/psum | solution.py:13
  281.0 484.7 %copy-start.7 = (f32[128,256]{1,0:T(8,128)}, f32[128,256]{1,0:T(8,128)S(1)}, u32[]{:S(2)}) copy-start(f32[128,256]{1,0:T(8,128)S(1)} %fusion.4) | copy-start | bytes 393220
  353.4 408.5 %all-reduce.9.cloned.1.call-start = ((), (), s32[]{:S(2)}) async-start(), calls=%async_computation.8 | async-start | bytes 1048576 | tf_op jit(solution)/shard_map/psum | solution.py:70
  609.5 156.2 %copy-start.5 = (f32[256,256]{1,0:T(8,128)}, f32[256,256]{1,0:T(8,128)S(1)}, u32[]{:S(2)}) copy-start(f32[256,256]{1,0:T(8,128)S(1)} %sub.23) | copy-start | bytes 786436
  763.3 2.4 copy-start.6
Sparse Core Ops, SparseCore 0:
  23.9 72.0 reduce-scatter.2
  98.4 111.1 all-gather.2
  213.5 66.1 reduce-scatter.4
  282.7 70.7 all-reduce.4
  355.7 114.4 all-gather.4
  472.5 135.9 all-reduce.6
  614.0 147.8 all-reduce.8
